TPU v7x, 32 devices: a whole 2x2x4 slice. The times are simulated.
32 devices in a mesh: dev: 8 (over z, y), rep: 4 (over x, core).
Axes of the slice: x: 2, y: 2, z: 4, core: 2. Of those that a mesh axis runs over, the one named last changes fastest.
Arguments:
- spins: int32 [8, 64], P('dev'), may hold values 0 or 1
- activations: float32 [4, 8, 64, 128], P('rep', 'dev'), may hold values from 0 to 0.5
- gradients: float32 [4, 8, 64, 256], P('rep', 'dev'), may hold values from -0.1 to 0.3
Outputs:
- gram: float32 [8, 8], P('dev', 'rep')
Inputs may be any that keep to these rules, and one draw needn't show every extreme that they name: `spins`: 1 marks an occupied site, 0 an empty one.
All inputs are finite; a program needn't handle non-finite values. No bound on the sum of `spins` on one device may be relied on, other than what follows from the above.
Results may differ from a plain program's by a relative error of at most 0.0001.
Values sent between devices are 32-bit elements; how exact they have to be, the bound alone decides.
No kernel may reach another device: no remote copies, remote signals or barrier semaphores. Data moves between devices by JAX's collectives and lax.ppermute only.
A program may use at most 128 MiB of HBM per device.

v0:
```python
import jax
import jax.numpy as jnp
from jax import lax
from jax.sharding import PartitionSpec as P


def form_scores(act, grad, occupied):
    weighted = act * occupied[None, :, :, None]
    score = jnp.einsum("psra,psrb->spab", weighted, grad, precision=lax.Precision.HIGHEST)
    return score.reshape(score.shape[0], score.shape[1], -1)


def body(spins, activations, gradients):
    occupied = spins.astype(jnp.float32)
    all_act, all_grad = (
        lax.all_gather(activations, "rep", axis=0, tiled=True),
        lax.all_gather(gradients, "rep", axis=0, tiled=True),
    )
    score = form_scores(all_act, all_grad, occupied)
    moved = lax.all_to_all(score, "dev", split_axis=2, concat_axis=0, tiled=True)
    total = moved.shape[0]
    centered = moved - jnp.mean(moved, axis=0, keepdims=True)
    width = total // lax.axis_size("rep")
    begin = lax.axis_index("rep") * width
    columns = lax.dynamic_slice_in_dim(centered, begin, width, 0)
    partial_gram = jnp.einsum("spa,tpa->st", centered, columns, precision=lax.Precision.HIGHEST)
    return lax.psum_scatter(partial_gram / total, "dev", scatter_dimension=0, tiled=True)


def solution(mesh):
    return jax.shard_map(
        body,
        mesh=mesh,
        in_specs=(P("dev", None), P("rep", "dev", None, None), P("rep", "dev", None, None)),
        out_specs=P("dev", "rep"),
        check_vma=False,
    )
```

profile of v0, /device:TPU:0, one launch (start us, length us, event | category | flops | bytes accessed | tf_op | source)
XLA Modules:
  0.0 278.7 jit_solution(6322244386527385481)
XLA Ops:
  0.0 7.4 %all_gather.7 = f32[4,1,64,256]{3,2,1,0:T(8,128)S(1)} all-gather(f32[1,1,64,256]{3,2,1,0:T(8,128)} %param.5), channel_id=1, replica_groups=mesh['dev'=8,'rep'=4] {'rep'}, dimensions={0}, use_global_device_ids=true | all-gather | bytes 327680 | tf_op jit(solution)/shard_map/all_gather | solution.py:17
  7.4 5.6 %all_gather.6 = f32[4,1,64,128]{3,2,1,0:T(8,128)S(1)} all-gather(f32[1,1,64,128]{3,2,1,0:T(8,128)} %param.4), channel_id=1, replica_groups=mesh['dev'=8,'rep'=4] {'rep'}, dimensions={0}, use_global_device_ids=true | all-gather | bytes 163840 | tf_op jit(solution)/shard_map/all_gather | solution.py:16
  13.0 0.7 convert_bitcast_fusion
  13.7 0.7 fusion.1
  14.4 8.7 %copy.7 = f32[4,128,256]{0,2,1:T(8,128)} copy(f32[4,128,256]{2,1,0:T(8,128)S(1)} %fusion.1) | data formatting | bytes 1048576 | tf_op jit(solution)/shard_map/reshape | solution.py:10
  23.1 0.5 broadcast.13
  23.6 146.5 %reduce.1 = f32[32768,4]{1,0:T(8,128)} reduce(f32[32768,1,4]{2,1,0:T(1,128)} %bitcast.23, f32[]{:T(128)} %broadcast.13), dimensions={1}, to_apply=%bitcast.20.reduce_sub_computation | reduce | bytes 1048580
  170.1 16.0 %reshape.23 = f32[8,1,16384]{2,1,0:T(1,128)} reshape(f32[32768,4]{1,0:T(8,128)} %reduce.1) | data formatting | bytes 1048576
  186.1 5.9 %all-to-all-start = ((f32[8,1,16384]{2,1,0:T(1,128)}), f32[8,1,16384]{2,1,0:T(1,128)S(1)}, u32[]{:S(2)}, u32[]{:S(2)}) async-start(f32[8,1,16384]{2,1,0:T(1,128)} %reshape.23), calls=%async_computation | async-start | bytes 1048576 | tf_op jit(solution)/shard_map/all_to_all | solution.py:20
  191.9 15.0 %all-to-all-done = f32[8,1,16384]{2,1,0:T(1,128)S(1)} async-done(((f32[8,1,16384]{2,1,0:T(1,128)}), f32[8,1,16384]{2,1,0:T(1,128)S(1)}, u32[]{:S(2)}, u32[]{:S(2)}) %all-to-all-start) | async-done | bytes 524320 | tf_op jit(solution)/shard_map/all_to_all | solution.py:20
  206.9 1.9 reduce.2
  208.8 0.0 copy-start
  208.8 37.3 %reshape.24 = f32[32768,1,4]{2,1,0:T(1,128)} reshape(f32[8,16384]{1,0:T(8,128)S(1)} %reduce.2) | data formatting | bytes 1048576
  246.1 9.8 %copy.8 = f32[1,4,8,4096]{3,2,1,0:T(8,128)S(1)} copy(f32[1,4,8,4096]{1,3,2,0:T(8,128)} %bitcast.24) | data formatting | bytes 1048576 | tf_op jit(solution)/shard_map/all_to_all | solution.py:20
  255.9 0.1 bitcast_reduce_fusion
  256.1 0.1 bitcast_subtract_fusion
  256.1 1.2 fusion
  257.3 0.0 copy-done
  257.3 0.7 dynamic-slice
  258.0 19.5 %all-reduce = f32[8,2]{1,0:T(8,128)S(1)} all-reduce(f32[8,2]{1,0:T(8,128)S(1)} %fusion), channel_id=2, replica_groups=mesh['dev'=8,'rep'=4] {'dev'}, use_global_device_ids=true, to_apply=%region_1.0.clone | all-reduce | flops 16 | bytes 128
  277.5 1.2 constant_dynamic-slice_fusion
  (1 shorter events, 0.0 us)
Async XLA Ops:
  186.1 20.9 %all-to-all-start = ((f32[8,1,16384]{2,1,0:T(1,128)}), f32[8,1,16384]{2,1,0:T(1,128)S(1)}, u32[]{:S(2)}, u32[]{:S(2)}) async-start(f32[8,1,16384]{2,1,0:T(1,128)} %reshape.23), calls=%async_computation | async-start | bytes 1048576 | tf_op jit(solution)/shard_map/all_to_all | solution.py:20
  208.8 48.5 %copy-start = (u32[32]{0:T(128)S(1)}, u32[32]{0:T(128)}, u32[]{:S(2)}) copy-start(u32[32]{0:T(128)} %constant.22) | copy-start | bytes 388
where the time goes:
time: 279 us
  other arithmetic  149 us (53%)
  local copies, waits for them, and re-layouts  74.1 us (27%)
  blocking collectives  32.5 us (12%)
  waiting for transfers between devices  15 us (5%)
  starting transfers between devices  5.88 us (2%)
    unnamed x1, other arithmetic  147 us
    unnamed x7, local copies, waits for them, and re-layouts  55.7 us
    unnamed x1, blocking collectives  19.5 us
    all_to_all x1, waiting for transfers between devices, body(): lax.all_to_all(score, 'dev', split_axis=2, concat_axis=0, tiled=True)  15 us
    all_to_all x1, local copies, waits for them, and re-layouts, body(): lax.all_to_all(score, 'dev', split_axis=2, concat_axis=0, tiled=True)  9.77 us
    reshape x1, local copies, waits for them, and re-layouts, form_scores(): return score.reshape(score.shape[0], score.shape[1], -1)  8.65 us
    all_gather x1, blocking collectives, body(): lax.all_gather(gradients, 'rep', axis=0, tiled=True)  7.42 us
    all_to_all x1, starting transfers between devices, body(): lax.all_to_all(score, 'dev', split_axis=2, concat_axis=0, tiled=True)  5.88 us
  transfers between devices with their start and end apart: 1, of which 1 were waited for; matrix products, arithmetic and copies ran while one was open for 0% of the time, Pallas kernels for 0%

commit v1 on v0

--- a/solution.py
+++ b/solution.py
@@ -17,7 +17,9 @@
         lax.all_gather(gradients, "rep", axis=0, tiled=True),
     )
     score = form_scores(all_act, all_grad, occupied)
-    moved = lax.all_to_all(score, "dev", split_axis=2, concat_axis=0, tiled=True)
+    moved = jnp.concatenate(
+        lax.all_to_all(jnp.stack(jnp.split(score, lax.axis_size("dev"), 2), axis=0), "dev", 0, 0), 0
+    )
     total = moved.shape[0]
     centered = moved - jnp.mean(moved, axis=0, keepdims=True)
     width = total // lax.axis_size("rep")

time: 279 us -> 63.3 us (0.23)
  other arithmetic: 149 us -> 0.42 us
  local copies, waits for them, and re-layouts: 74.1 us -> 7.15 us
    unnamed x1 -> x0, other arithmetic: 147 us -> none
    unnamed x7 -> x15, local copies, waits for them, and re-layouts: 55.7 us -> 6.27 us
    all_to_all x1 -> x0, local copies, waits for them, and re-layouts: 9.77 us -> none  [body(): lax.all_to_all(score, 'dev', split_axis=2, concat_axis=0, tiled=True)]
    reshape x1, local copies, waits for them, and re-layouts: 8.65 us -> 0.26 us  [form_scores(): return score.reshape(score.shape[0], score.shape[1], -1)]
where the time goes in v1:
time: 63.3 us; the launch traced here: 63 us
  blocking collectives  32.5 us (51%)
  waiting for transfers between devices  15 us (24%)
  local copies, waits for them, and re-layouts  7.15 us (11%)
  starting transfers between devices  5.86 us (9%)
  matrix products  1.93 us (3%)
    unnamed x1, blocking collectives  19.5 us
    all_to_all x1, waiting for transfers between devices, body(): lax.all_to_all(jnp.stack(jnp.split(score, lax.axis_size('dev'), 2), axis=...  15 us
    all_gather x1, blocking collectives, body(): lax.all_gather(gradients, 'rep', axis=0, tiled=True)  7.55 us
    unnamed x15, local copies, waits for them, and re-layouts  6.27 us
    all_to_all x1, starting transfers between devices, body(): lax.all_to_all(jnp.stack(jnp.split(score, lax.axis_size('dev'), 2), axis=...  5.86 us
    all_gather x1, blocking collectives, body(): lax.all_gather(activations, 'rep', axis=0, tiled=True)  5.53 us
  transfers between devices with their start and end apart: 1, of which 1 were waited for; matrix products, arithmetic and copies ran while one was open for 0% of the time, Pallas kernels for 0%

profile of v1, /device:TPU:0, one launch (start us, length us, event | category | flops | bytes accessed | tf_op | source)
XLA Modules:
  0.0 63.0 jit_solution(13747785996527098711)
XLA Ops:
  0.0 0.0 copy-start
  0.0 7.5 %all_gather.7 = f32[4,1,64,256]{3,2,1,0:T(8,128)S(1)} all-gather(f32[1,1,64,256]{3,2,1,0:T(8,128)} %param.5), channel_id=1, replica_groups=mesh['dev'=8,'rep'=4] {'rep'}, dimensions={0}, use_global_device_ids=true | all-gather | bytes 327680 | tf_op jit(solution)/shard_map/all_gather | solution.py:17
  7.6 0.0 copy-done
  7.6 0.0 copy-start.1
  7.6 5.5 %all_gather.6 = f32[4,1,64,128]{3,2,1,0:T(8,128)S(1)} all-gather(f32[1,1,64,128]{3,2,1,0:T(8,128)S(1)} %copy-done), channel_id=1, replica_groups=mesh['dev'=8,'rep'=4] {'rep'}, dimensions={0}, use_global_device_ids=true | all-gather | bytes 163840 | tf_op jit(solution)/shard_map/all_gather | solution.py:16
  13.1 0.0 copy-done.1
  13.1 0.7 %fusion.1 = f32[4,128,256]{2,1,0:T(8,128)S(1)} fusion(f32[4,1,64,256]{3,2,1,0:T(8,128)S(1)} %all_gather.7, f32[4,1,64,128]{3,2,1,0:T(8,128)S(1)} %all_gather.6, f32[64]{0:T(128)S(1)} %convert_bitcast_fusion), kind=kOutput, calls=%fused_computation.3 | convolution fusion | flops 100696064 | bytes 917760 | tf_op jit(solution)/shard_map/psra,psrb->spab/dot_general | solution.py:9
  13.8 0.3 reshape.23
  14.1 0.6 fusion.13
  14.7 0.6 fusion.12
  15.3 0.6 fusion.11
  15.9 0.6 fusion.10
  16.6 0.6 fusion.9
  17.2 0.6 %fusion.8 = f32[8,1,4,4096]{3,2,1,0:T(4,128)} fusion(f32[8,1,4,4096]{3,2,1,0:T(4,128)} %fusion.9, f32[1,4,32768]{2,1,0:T(4,128)S(1)} %reshape.23), kind=kLoop, calls=%fused_computation.13 | loop fusion | bytes 131072
  17.8 0.6 fusion.7
  18.4 0.6 fusion.6
  19.1 5.9 %all-to-all-start = ((f32[8,1,4,4096]{3,2,1,0:T(4,128)}), f32[8,1,4,4096]{3,2,1,0:T(4,128)S(1)}, u32[]{:S(2)}, u32[]{:S(2)}) async-start(f32[8,1,4,4096]{3,2,1,0:T(4,128)} %fusion.6), calls=%async_computation | async-start | bytes 1048576 | tf_op jit(solution)/shard_map/all_to_all | solution.py:21
  24.9 15.0 %all-to-all-done = f32[8,1,4,4096]{3,2,1,0:T(4,128)S(1)} async-done(((f32[8,1,4,4096]{3,2,1,0:T(4,128)}), f32[8,1,4,4096]{3,2,1,0:T(4,128)S(1)}, u32[]{:S(2)}, u32[]{:S(2)}) %all-to-all-start) | async-done | bytes 524320 | tf_op jit(solution)/shard_map/all_to_all | solution.py:21
  39.9 0.1 reduce_sum.9
  40.0 0.3 bitcast_subtract_fusion
  40.4 0.0 copy-start.2
  40.4 1.2 %fusion = f32[8,2]{1,0:T(8,128)S(1)} fusion(f32[8,4,4096]{2,0,1:T(8,128)S(1)} %bitcast_subtract_fusion, s32[]{:T(128)S(6)} %select_n.3), kind=kOutput, calls=%fused_computation.1 | convolution fusion | flops 3145744 | bytes 655428 | tf_op jit(solution)/shard_map/spa,tpa->st/dot_general | solution.py:28
  41.6 0.0 copy-done.2
  41.6 0.7 %dynamic-slice = u32[1]{0:T(128)} dynamic-slice(u32[32]{0:T(128)S(1)} %copy-done.2, u32[]{:T(128)S(6)} %add.7), dynamic_slice_sizes={1} | dynamic-slice | bytes 12
  42.3 19.5 %all-reduce = f32[8,2]{1,0:T(8,128)S(1)} all-reduce(f32[8,2]{1,0:T(8,128)S(1)} %fusion), channel_id=2, replica_groups=mesh['dev'=8,'rep'=4] {'dev'}, use_global_device_ids=true, to_apply=%region_1.0.clone | all-reduce | flops 16 | bytes 128
  61.8 1.2 %constant_dynamic-slice_fusion = f32[1,2]{1,0:T(1,128)} fusion(f32[8,2]{1,0:T(8,128)S(1)} %all-reduce, u32[]{:T(128)} %bitcast.13), kind=kLoop, calls=%fused_computation.26 | loop fusion | bytes 20
  (2 shorter events, 0.0 us)
Async XLA Ops:
  0.0 7.6 %copy-start = (f32[1,1,64,128]{3,2,1,0:T(8,128)S(1)}, f32[1,1,64,128]{3,2,1,0:T(8,128)}, u32[]{:S(2)}) copy-start(f32[1,1,64,128]{3,2,1,0:T(8,128)} %param.4) | copy-start | bytes 98308
  7.6 5.5 %copy-start.1 = (s32[1,64]{1,0:T(1,128)S(1)}, s32[1,64]{1,0:T(1,128)}, u32[]{:S(2)}) copy-start(s32[1,64]{1,0:T(1,128)} %param.3) | copy-start | bytes 772
  19.1 20.9 %all-to-all-start = ((f32[8,1,4,4096]{3,2,1,0:T(4,128)}), f32[8,1,4,4096]{3,2,1,0:T(4,128)S(1)}, u32[]{:S(2)}, u32[]{:S(2)}) async-start(f32[8,1,4,4096]{3,2,1,0:T(4,128)} %fusion.6), calls=%async_computation | async-start | bytes 1048576 | tf_op jit(solution)/shard_map/all_to_all | solution.py:21
  40.4 1.2 %copy-start.2 = (u32[32]{0:T(128)S(1)}, u32[32]{0:T(128)}, u32[]{:S(2)}) copy-start(u32[32]{0:T(128)} %constant.22) | copy-start | bytes 388
